TPU v7x, 128 devices: a whole 4x4x4 slice. The times are simulated.
128 devices in a mesh: tm: 8 (over z, x_hi), docs: 16 (over y, x_lo, core).
Axes of the slice: x: 4 (x_hi: 2, x_lo: 2; x = x_hi * 2 + x_lo), y: 4, z: 4, core: 2. Of those that a mesh axis runs over, the one named last changes fastest.
Arguments:
- counts: int32 [8, 1024, 32768], P('tm', 'docs'), may hold values from 0 to 5, as said below
- topic_means: float32 [8, 32768, 128], P('tm', 'docs'), may hold values from -80 to 170
- doc_topics_init: float32 [8, 1024, 128], P('tm', 'docs'), may hold values from 0.5 to 20
- dirichlet_prior: float32 [128], replicated, may hold values from 0.05 to 1
- chain_var: float32 [128], replicated, may hold values from 0.005 to 0.5
- obs_noise: float32 [128], replicated, may hold values from 0.1 to 10
Outputs:
- smoothed_means: float32 [8, 32768, 128], P('tm', 'docs')
- doc_topics: float32 [8, 1024, 128], P('tm', 'docs')
Inputs may be any that keep to these rules, and one draw needn't show every extreme that they name: `counts`: each entry is 0 or a count of 1 to 5; each word has its own share of nonzero entries, between a quarter and three quarters.
All inputs are finite; a program needn't handle non-finite values.
Results may differ from a plain program's by a relative error of at most 0.01.
Values may be sent and summed in bfloat16 or wider, within the bound.
No kernel may reach another device: no remote copies, remote signals or barrier semaphores. Data moves between devices by JAX's collectives and lax.ppermute only.
A program may use at most 128 MiB of HBM per device.

v0:
```python
import jax
import jax.numpy as jnp
from jax import lax
from jax.sharding import Mesh
from jax.sharding import PartitionSpec as P

V = 32768
ITERS_E = 4
TM = ("tm_0", "tm_1")
TM_DOCS = ("tm_0", "tm_1", "docs")
prior_count = 0.5
initial_scale = 1000.0


def merged(part, axis, combine):
    gathered = jax.tree.map(lambda a: lax.all_gather(a, axis), part)

    def take(source):
        return jax.tree.map(lambda a: lax.dynamic_index_in_dim(a, source, 0, False), gathered)

    return lax.fori_loop(
        1, lax.axis_size(axis), lambda source, state: combine(state, take(source)), take(0)
    )


def filled_with(shard, identity):
    return jax.tree.map(
        lambda a, e: jnp.broadcast_to(jnp.asarray(e, a.dtype), a.shape), shard, identity
    )


def carried_in(shard, axes, combine, identity):
    before = start = filled_with(shard, identity)
    subtotal = shard
    for axis in reversed(axes):
        devices, place = (lax.axis_size(axis), lax.axis_index(axis))
        pieces = jax.tree.map(
            lambda part, kind: lax.all_gather(part.astype(kind), axis),
            subtotal,
            (jnp.bfloat16, jnp.bfloat16),
        )
        inside, subtotal = (start, start)
        for k in range(devices):
            passed = k < place
            subtotal = combine(
                subtotal, jax.tree.map(lambda part, own: part[k].astype(own.dtype), pieces, shard)
            )
            inside = jax.tree.map(lambda new, old: jnp.where(passed, new, old), subtotal, inside)
        before = combine(inside, before)
    return before


def prefix_by_axis(shard, axes, combine, identity):
    before = start = filled_with(shard, identity)
    subtotal = shard
    for axis in reversed(axes):
        devices, place = (lax.axis_size(axis), lax.axis_index(axis))
        pieces = jax.tree.map(
            lambda part, kind: lax.all_gather(part.astype(kind), axis),
            subtotal,
            jax.tree.map(lambda a: jnp.bfloat16 if a.dtype == jnp.float32 else a.dtype, shard),
        )
        inside, subtotal = (start, start)
        for k in reversed(range(devices)):
            passed = k > place
            subtotal = combine(
                subtotal, jax.tree.map(lambda part, own: part[k].astype(own.dtype), pieces, shard)
            )
            inside = jax.tree.map(lambda new, old: jnp.where(passed, new, old), subtotal, inside)
        before = combine(inside, before)
    return before


def chain_factors(totals, chain_var, obs_noise):
    relative = jnp.sum(totals, axis=1, keepdims=True) / (totals.shape[1] * totals)
    noise = obs_noise[None, :] * relative

    def advance(previous, noise_level):
        predicted = previous + chain_var
        own_gain = predicted / (predicted + noise_level)
        current = (1.0 - own_gain) * predicted
        return (current, (own_gain, current))

    unused, (gains, filtered_var) = lax.scan(advance, initial_scale * chain_var, noise)
    smooth = filtered_var / (filtered_var + chain_var)
    smooth = jnp.concatenate([smooth[:-1], jnp.zeros_like(smooth[-1:])], axis=0)
    return (gains, smooth)


def compose(former, latter):
    return (former[0] * latter[0], latter[0] * former[1] + latter[1])


def join_mass(former, latter):
    highest = jnp.maximum(former[0], latter[0])
    return (
        highest,
        former[1] * jnp.exp(former[0] - highest) + latter[1] * jnp.exp(latter[0] - highest),
    )


def body(counts, topic_means, doc_topics_init, dirichlet_prior, chain_var, obs_noise):
    topic_slab = topic_means[0]
    concentration = doc_topics_init[0]
    count_wide = counts[0].astype(jnp.float32)
    local_peak = jnp.max(topic_slab, axis=0)
    local_mass = jnp.sum(jnp.exp(topic_slab - local_peak[None, :]), axis=0)
    column_peak, column_mass = merged((local_peak, local_mass), "docs", join_mass)
    beta_slab = jnp.exp(topic_slab - (column_peak + jnp.log(column_mass))[None, :]).astype(
        jnp.bfloat16
    )
    beta_full = lax.all_gather(beta_slab, "docs", axis=0, tiled=True)
    for sweep_index in range(ITERS_E):
        proportions = jnp.exp(lax.digamma(concentration)).astype(jnp.bfloat16)
        mixture = lax.dot_general(
            proportions, beta_full, (((1,), (1,)), ((), ())), preferred_element_type=jnp.float32
        )
        ratios = (count_wide / mixture).astype(jnp.bfloat16)
        update = proportions.astype(jnp.float32) * jnp.dot(
            ratios, beta_full, preferred_element_type=jnp.float32
        )
        concentration = dirichlet_prior[None, :] + update
    word_stats = lax.psum_scatter(
        (
            beta_full.astype(jnp.float32)
            * lax.dot_general(
                ratios, proportions, (((0,), (0,)), ((), ())), preferred_element_type=jnp.float32
            )
        ).astype(jnp.bfloat16),
        "docs",
        scatter_dimension=0,
        tiled=True,
    ).astype(jnp.float32)
    slice_index = lax.axis_index(TM)
    slices = lax.axis_size(TM)
    own_row = (jnp.arange(slices) == slice_index).astype(jnp.float32)
    placed = own_row[:, None] * jnp.sum(update, axis=0)[None, :]
    totals = lax.psum(placed, TM_DOCS)
    gains, smooth = chain_factors(totals, chain_var, obs_noise)
    own_total = jnp.sum(own_row[:, None] * totals, axis=0)
    own_gain = jnp.sum(own_row[:, None] * gains, axis=0)
    own_factor = jnp.sum(own_row[:, None] * smooth, axis=0)
    pseudo = jnp.log(word_stats + prior_count) - jnp.log((own_total + prior_count * V) / V)[None, :]
    forward_rate = 1.0 - own_gain
    forward_term = own_gain[None, :] * pseudo
    neutral = (jnp.ones_like(forward_rate), jnp.zeros_like(forward_term))
    entering = carried_in((forward_rate, forward_term), TM, compose, neutral)[1]
    filtered = forward_rate[None, :] * entering + forward_term
    back_term = (1.0 - own_factor)[None, :] * filtered
    following = prefix_by_axis((own_factor, back_term), TM, compose, neutral)[1]
    smoothed = own_factor[None, :] * following + back_term
    return (smoothed[None], concentration[None])


def solution(mesh):
    split = Mesh(mesh.devices.reshape(4, 2, mesh.shape["docs"]), ("tm_0", "tm_1", "docs"))
    placed = (P(TM, "docs", None), P(TM, "docs", None), P(TM, "docs", None), P(), P(), P())
    return jax.shard_map(
        body,
        mesh=split,
        in_specs=placed,
        out_specs=(P(TM, "docs", None), P(TM, "docs", None)),
        check_vma=False,
    )
```

profile of v0, /device:TPU:1, one launch (start us, length us, event | category | flops | bytes accessed | tf_op | source)
XLA Modules:
  0.0 390.9 jit_solution(17476896300496999206)
XLA Ops:
  10.2 21.2 %all-gather.7 = f32[16,1,128]{2,1,0:T(1,128)S(1)} all-gather(f32[1,1,128]{2,1,0:T(1,128)S(1)} %bitcast.319), channel_id=3, replica_groups=mesh['tm_0'=4,'tm_1'=2,'docs'=16] {'docs'}, dimensions={0}, use_global_device_ids=true | all-gather | bytes 8704 | tf_op jit(solution)/shard_map/all_gather | solution.py:16
  31.4 16.3 %all-gather.6 = f32[16,1,128]{2,1,0:T(1,128)S(1)} all-gather(f32[1,1,128]{2,1,0:T(1,128)S(1)} %bitcast.318), channel_id=2, replica_groups=mesh['tm_0'=4,'tm_1'=2,'docs'=16] {'docs'}, dimensions={0}, use_global_device_ids=true | all-gather | bytes 8704 | tf_op jit(solution)/shard_map/all_gather | solution.py:16
  48.4 2.2 fusion.53
  50.6 51.7 %all-gather.18.cloned.1.call-done = bf16[32768,128]{1,0:T(8,128)(2,1)} async-done(((bf16[2048,128]{1,0:T(8,128)(2,1)}), bf16[32768,128]{1,0:T(8,128)(2,1)}) %all-gather.18.cloned.1.call-update) | async-done | bytes 8388624 | tf_op jit(solution)/shard_map/all_gather | solution.py:112
  102.3 13.1 %fusion.62 = bf16[64,128]{1,0:T(8,128)(2,1)S(1)} fusion(bf16[32768,128]{1,0:T(8,128)(2,1)} %all-gather.18.cloned.1.call-done, s32[1,64,32768]{2,1,0:T(8,128)} %param.10, f32[1,64,128]{2,1,0:T(8,128)} %param.12, f32[128]{0:T(128)} %param.13), kind=kOutput, calls=%fused_computation.109 | convolution fusion | flops 1081925632 | bytes 16826880 | tf_op jit(solution)/shard_map/dot_general | solution.py:119
  115.4 12.6 %fusion.66 = bf16[64,128]{1,0:T(8,128)(2,1)S(1)} fusion(bf16[32768,128]{1,0:T(8,128)(2,1)} %all-gather.18.cloned.1.call-done, bf16[64,128]{1,0:T(8,128)(2,1)S(1)} %fusion.62, s32[1,64,32768]{2,1,0:T(8,128)} %param.10, f32[128]{0:T(128)S(1)} %copy-done.2), kind=kOutput, calls=%fused_computation.113 | convolution fusion | flops 1080680448 | bytes 16810496 | tf_op jit(solution)/shard_map/dot_general | solution.py:119
  128.0 12.4 %fusion.15 = f32[64,128]{1,0:T(8,128)S(1)} fusion(bf16[32768,128]{1,0:T(8,128)(2,1)} %all-gather.18.cloned.1.call-done, bf16[64,128]{1,0:T(8,128)(2,1)S(1)} %fusion.66, s32[1,64,32768]{2,1,0:T(8,128)} %param.10, f32[128]{0:T(128)S(1)} %copy-done.2), kind=kOutput, calls=%fused_computation.35 | convolution fusion | flops 1080057856 | bytes 16826880 | tf_op jit(solution)/shard_map/dot_general | solution.py:119
  140.4 9.2 %fusion.3 = bf16[64,32768]{1,0:T(8,128)(2,1)S(1)} fusion(bf16[32768,128]{1,0:T(8,128)(2,1)} %all-gather.18.cloned.1.call-done, s32[1,64,32768]{2,1,0:T(8,128)} %param.10, f32[64,128]{1,0:T(8,128)S(1)} %fusion.15), kind=kOutput, calls=%fused_computation.11 | convolution fusion | flops 543784960 | bytes 21004288 | tf_op jit(solution)/shard_map/dot_general | solution.py:115
  151.5 7.3 %fusion.2 = bf16[32768,128]{1,0:T(8,128)(2,1)} fusion(bf16[64,32768]{1,0:T(8,128)(2,1)S(1)} %fusion.3, bf16[32768,128]{1,0:T(8,128)(2,1)} %all-gather.18.cloned.1.call-done, f32[64,128]{1,0:T(8,128)S(1)} %fusion.15), kind=kOutput, calls=%fused_computation.9 | convolution fusion | flops 550076416 | bytes 21004288 | tf_op jit(solution)/shard_map/dot_general | solution.py:126
  159.5 7.0 %add_bitcast_fusion = (f32[1,64,128]{2,1,0:T(8,128)}, f32[128]{0:T(128)S(1)}) fusion(f32[128]{0:T(128)S(1)} %copy-done.2, bf16[64,32768]{1,0:T(8,128)(2,1)} %copy-done, bf16[32768,128]{1,0:T(8,128)(2,1)} %all-gather.18.cloned.1.call-done, f32[64,128]{1,0:T(8,128)S(1)} %fusion.15), kind=kOutput, calls=%fused_computation.129 | convolution fusion | flops 537526144 | bytes 12649472 | tf_op jit(solution)/shard_map/dot_general | solution.py:119
  166.6 67.0 %psum.7 = f32[8,128]{1,0:T(8,128)S(1)} all-reduce(f32[8,128]{1,0:T(8,128)S(1)} %broadcast_multiply_fusion), channel_id=1, replica_groups=mesh['tm_0'=4,'tm_1'=2,'docs'=16] {'tm_0','tm_1','docs'}, use_global_device_ids=true, to_apply=%region_5.6 | all-reduce | flops 1024 | bytes 8192 | tf_op jit(solution)/shard_map/psum | solution.py:138
  234.8 22.3 %reduce-scatter.2.cloned.1.call-done = bf16[2048,128]{1,0:T(8,128)(2,1)} async-done(((bf16[32768,128]{1,0:T(8,128)(2,1)}), bf16[2048,128]{1,0:T(8,128)(2,1)}) %reduce-scatter.2.cloned.1.call-update) | async-done | bytes 524304 | tf_op jit(solution)/shard_map/reduce_scatter | solution.py:123
  259.3 4.6 %all-gather.10 = bf16[2,1,128]{2,1,0:T(2,128)(2,1)S(1)} all-gather(bf16[1,1,128]{2,1,0:T(2,128)(2,1)S(1)} %get-tuple-element.221), channel_id=5, replica_groups=mesh['tm_0'=4,'tm_1'=2,'docs'=16] {'tm_1'}, dimensions={0}, use_global_device_ids=true | all-gather | bytes 768 | tf_op jit(solution)/shard_map/all_gather | solution.py:38
  263.9 21.5 %all-gather.24.cloned.1.call-done = bf16[4096,128]{1,0:T(8,128)(2,1)} async-done(((bf16[2048,128]{1,0:T(8,128)(2,1)}), bf16[4096,128]{1,0:T(8,128)(2,1)}) %all-gather.24.cloned.1.call-update) | async-done | bytes 1048592 | tf_op jit(solution)/shard_map/all_gather | solution.py:38
  285.4 2.2 fusion.33
  287.7 7.9 %all-gather.11 = bf16[4,1,128]{2,1,0:T(2,128)(2,1)S(1)} all-gather(bf16[1,1,128]{2,1,0:T(2,128)(2,1)S(1)} %get-tuple-element.216), channel_id=1, replica_groups=mesh['tm_0'=4,'tm_1'=2,'docs'=16] {'tm_0'}, dimensions={0}, use_global_device_ids=true | all-gather | bytes 1280 | tf_op jit(solution)/shard_map/all_gather | solution.py:38
  295.6 22.6 %all-gather.20.cloned.1.call-done = bf16[4,2048,128]{2,1,0:T(8,128)(2,1)} async-done(((bf16[1,2048,128]{2,1,0:T(8,128)(2,1)}), bf16[4,2048,128]{2,1,0:T(8,128)(2,1)}) %all-gather.20.cloned.1.call-update) | async-done | bytes 2097168 | tf_op jit(solution)/shard_map/all_gather | solution.py:38
  318.2 3.9 %fusion.309 = (bf16[2048,128]{1,0:T(8,128)(2,1)}, f32[2048,128]{1,0:T(8,128)S(1)}) fusion(f32[128]{0:T(128)S(1)} %multiply_log_fusion, bf16[2048,128]{1,0:T(8,128)(2,1)} %reduce-scatter.2.cloned.1.call-done, f32[128]{0:T(128)S(1)} %get-tuple-element.175, pred[]{:T(512)S(6)} %gt.19, bf16[4096,128]{1,0:T(8,128)(2,1)} %all-gather.24.cloned.1.call-done, ...), kind=kLoop, calls=%fused_computation.345 | loop fusion | flops 8388608 | bytes 5248518 | tf_op jit(solution)/shard_map/convert_element_type | solution.py:59
  322.2 4.6 %all-gather.8 = bf16[2,1,128]{2,1,0:T(2,128)(2,1)S(1)} all-gather(bf16[1,1,128]{2,1,0:T(2,128)(2,1)S(1)} %get-tuple-element.218), channel_id=4, replica_groups=mesh['tm_0'=4,'tm_1'=2,'docs'=16] {'tm_1'}, dimensions={0}, use_global_device_ids=true | all-gather | bytes 768 | tf_op jit(solution)/shard_map/all_gather | solution.py:59
  326.8 20.7 %all-gather.26.cloned.1.call-done = bf16[4096,128]{1,0:T(8,128)(2,1)} async-done(((bf16[2048,128]{1,0:T(8,128)(2,1)}), bf16[4096,128]{1,0:T(8,128)(2,1)}) %all-gather.26.cloned.1.call-update) | async-done | bytes 1048592 | tf_op jit(solution)/shard_map/all_gather | solution.py:59
  347.5 2.2 fusion.37
  349.7 7.9 %all-gather.9 = bf16[4,1,128]{2,1,0:T(2,128)(2,1)S(1)} all-gather(bf16[1,1,128]{2,1,0:T(2,128)(2,1)S(1)} %get-tuple-element.212), channel_id=1, replica_groups=mesh['tm_0'=4,'tm_1'=2,'docs'=16] {'tm_0'}, dimensions={0}, use_global_device_ids=true | all-gather | bytes 1280 | tf_op jit(solution)/shard_map/all_gather | solution.py:59
  357.6 22.7 %all-gather.22.cloned.1.call-done = bf16[4,2048,128]{2,1,0:T(8,128)(2,1)} async-done(((bf16[1,2048,128]{2,1,0:T(8,128)(2,1)}), bf16[4,2048,128]{2,1,0:T(8,128)(2,1)}) %all-gather.22.cloned.1.call-update) | async-done | bytes 2097168 | tf_op jit(solution)/shard_map/all_gather | solution.py:59
  380.3 3.7 fusion.24
  (88 shorter events, 11.0 us)
Async XLA Ops:
  7.2 95.1 %all-gather.18.cloned.1.call-start = ((), (), s32[]{:S(2)}) async-start(), calls=%async_computation.1 | async-start | bytes 8912896 | tf_op jit(solution)/shard_map/all_gather | solution.py:112
  50.6 64.9 %copy-start.2 = (f32[128]{0:T(128)S(1)}, f32[128]{0:T(128)}, u32[]{:S(2)}) copy-start(f32[128]{0:T(128)} %param.13) | copy-start | bytes 1540
  50.6 206.5 %reduce-scatter.2.cloned.1.call-start = ((), (), s32[]{:S(2)}) async-start(), calls=%async_computation.2 | async-start | bytes 8912896 | tf_op jit(solution)/shard_map/reduce_scatter | solution.py:123
  149.6 1.9 copy-start
  158.8 0.7 copy-start.1
  158.9 126.5 %all-gather.24.cloned.1.call-start = ((), (), s32[]{:S(2)}) async-start(), calls=%async_computation.5 | async-start | bytes 1572864 | tf_op jit(solution)/shard_map/all_gather | solution.py:38
  159.5 74.2 %copy-start.3 = (f32[128]{0:T(128)S(1)}, f32[128]{0:T(128)}, u32[]{:S(2)}) copy-start(f32[128]{0:T(128)} %param.15) | copy-start | bytes 1540
  159.5 75.2 %copy-start.4 = (pred[8]{0:T(512)(128)(4,1)S(1)}, pred[8]{0:T(512)(128)(4,1)}, u32[]{:S(2)}) copy-start(pred[8]{0:T(512)(128)(4,1)} %constant.117.clone.1) | copy-start | bytes 28
  259.2 59.0 %all-gather.20.cloned.1.call-start = ((), (), s32[]{:S(2)}) async-start(), calls=%async_computation.3 | async-start | bytes 2621440 | tf_op jit(solution)/shard_map/all_gather | solution.py:38
  287.6 59.9 %all-gather.26.cloned.1.call-start = ((), (), s32[]{:S(2)}) async-start(), calls=%async_computation.6 | async-start | bytes 1572864 | tf_op jit(solution)/shard_map/all_gather | solution.py:59
  322.2 58.1 %all-gather.22.cloned.1.call-start = ((), (), s32[]{:S(2)}) async-start(), calls=%async_computation.4 | async-start | bytes 2621440 | tf_op jit(solution)/shard_map/all_gather | solution.py:59
Sparse Core Ops, SparseCore 0:
  50.7 51.5 all-gather.17
  159.0 98.0 reduce-scatter.1
  259.3 26.0 all-gather.23
  287.7 30.4 all-gather.19
  322.3 25.1 all-gather.25
  349.8 30.4 all-gather.21
where the time goes:
time: 391 us
  waiting for transfers between devices  162 us (41%)
  blocking collectives  129 us (33%)
  matrix products  61.6 us (16%)
  other arithmetic  20.3 us (5%)
  between operations  14.3 us (4%)
    psum x1, blocking collectives, body(): totals = lax.psum(placed, TM_DOCS)  67 us
    all_gather x1, waiting for transfers between devices, body(): beta_full = lax.all_gather(beta_slab, 'docs', axis=0, tiled=True)  51.7 us
    dot_general x4, matrix products, body(): jnp.dot(ratios, beta_full, preferred_element_type=jnp.float32)  45.1 us
    all_gather x2, waiting for transfers between devices, carried_in(): lax.all_gather(part.astype(kind), axis)  44.2 us
    all_gather x2, waiting for transfers between devices, prefix_by_axis(): lax.all_gather(part.astype(kind), axis)  43.4 us
    all_gather x2, blocking collectives, merged(): gathered = jax.tree.map(lambda a: lax.all_gather(a, axis), part)  37.5 us
    reduce_scatter x1, waiting for transfers between devices, body(): lax.psum_scatter((beta_full.astype(jnp.float32) * lax.dot_general(ratios,...  22.3 us
    all_gather x2, blocking collectives, carried_in(): lax.all_gather(part.astype(kind), axis)  12.5 us
  transfers between devices with their start and end apart: 6, of which 6 were waited for; matrix products, arithmetic and copies ran while one was open for 2% of the time, Pallas kernels for 0%

commit v1 on v0

--- a/solution.py
+++ b/solution.py
@@ -109,7 +109,9 @@
     beta_slab = jnp.exp(topic_slab - (column_peak + jnp.log(column_mass))[None, :]).astype(
         jnp.bfloat16
     )
-    beta_full = lax.all_gather(beta_slab, "docs", axis=0, tiled=True)
+    beta_full = jnp.concatenate(
+        lax.all_to_all(jnp.stack([beta_slab] * lax.axis_size("docs")), "docs", 0, 0), axis=0
+    )
     for sweep_index in range(ITERS_E):
         proportions = jnp.exp(lax.digamma(concentration)).astype(jnp.bfloat16)
         mixture = lax.dot_general(

time: 391 us -> 437 us (1.12)
  blocking collectives: 129 us -> 227 us
  waiting for transfers between devices: 162 us -> 110 us
    all_to_all x0 -> x1, blocking collectives: none -> 97.5 us  [body(): lax.all_to_all(jnp.stack([beta_slab] * lax.axis_size('docs')), 'docs', 0, 0)]
    all_gather x1 -> x0, waiting for transfers between devices: 51.7 us -> none  [body(): beta_full = lax.all_gather(beta_slab, 'docs', axis=0, tiled=True)]
  transfers between devices with their start and end apart: 6 -> 5, of which waited for: 6 -> 5; matrix products, arithmetic and copies ran while one was open for 2% -> 2% of each run, Pallas kernels for 0% -> 0%
where the time goes in v1:
time: 437 us
  blocking collectives  227 us (52%)
  waiting for transfers between devices  110 us (25%)
  matrix products  61.6 us (14%)
  other arithmetic  19.5 us (4%)
  between operations  14 us (3%)
  local copies, waits for them, and re-layouts  4.66 us (1%)
    all_to_all x1, blocking collectives, body(): lax.all_to_all(jnp.stack([beta_slab] * lax.axis_size('docs')), 'docs', 0, 0)  97.5 us
    psum x1, blocking collectives, body(): totals = lax.psum(placed, TM_DOCS)  66.8 us
    dot_general x4, matrix products, body(): jnp.dot(ratios, beta_full, preferred_element_type=jnp.float32)  45.1 us
    all_gather x2, waiting for transfers between devices, carried_in(): lax.all_gather(part.astype(kind), axis)  44.1 us
    all_gather x2, waiting for transfers between devices, prefix_by_axis(): lax.all_gather(part.astype(kind), axis)  43.4 us
    all_gather x2, blocking collectives, merged(): gathered = jax.tree.map(lambda a: lax.all_gather(a, axis), part)  37.5 us
    reduce_scatter x1, waiting for transfers between devices, body(): lax.psum_scatter((beta_full.astype(jnp.float32) * lax.dot_general(ratios,...  22.2 us
    all_gather x2, blocking collectives, carried_in(): lax.all_gather(part.astype(kind), axis)  12.5 us
  transfers between devices with their start and end apart: 5, of which 5 were waited for; matrix products, arithmetic and copies ran while one was open for 2% of the time, Pallas kernels for 0%

profile of v1, /device:TPU:1, one launch (start us, length us, event | category | flops | bytes accessed | tf_op | source)
XLA Modules:
  0.0 436.9 jit_solution(6214261179668147207)
XLA Ops:
  10.2 21.2 %all-gather.7 = f32[16,1,128]{2,1,0:T(1,128)S(1)} all-gather(f32[1,1,128]{2,1,0:T(1,128)S(1)} %bitcast.324), channel_id=3, replica_groups=mesh['tm_0'=4,'tm_1'=2,'docs'=16] {'docs'}, dimensions={0}, use_global_device_ids=true | all-gather | bytes 8704 | tf_op jit(solution)/shard_map/all_gather | solution.py:16
  31.4 16.3 %all-gather.6 = f32[16,1,128]{2,1,0:T(1,128)S(1)} all-gather(f32[1,1,128]{2,1,0:T(1,128)S(1)} %bitcast.323), channel_id=2, replica_groups=mesh['tm_0'=4,'tm_1'=2,'docs'=16] {'docs'}, dimensions={0}, use_global_device_ids=true | all-gather | bytes 8704 | tf_op jit(solution)/shard_map/all_gather | solution.py:16
  51.4 97.5 %all_to_all.5 = bf16[16,2048,128]{2,1,0:T(8,128)(2,1)} all-to-all(bf16[16,2048,128]{2,1,0:T(8,128)(2,1)S(1)} %stack.5), channel_id=1, replica_groups=mesh['tm_0'=4,'tm_1'=2,'docs'=16] {'docs'}, dimensions={0} | all-to-all | bytes 16777216 | tf_op jit(solution)/shard_map/all_to_all | solution.py:113
  148.9 13.1 %fusion.65 = bf16[64,128]{1,0:T(8,128)(2,1)S(1)} fusion(bf16[32768,128]{1,0:T(8,128)(2,1)} %bitcast.313, s32[1,64,32768]{2,1,0:T(8,128)} %param.10, f32[1,64,128]{2,1,0:T(8,128)S(1)} %copy-done.5, f32[128]{0:T(128)S(1)} %copy-done.2), kind=kOutput, calls=%fused_computation.114 | convolution fusion | flops 1081925632 | bytes 16826880 | tf_op jit(solution)/shard_map/dot_general | solution.py:121
  162.0 12.6 %fusion.69 = bf16[64,128]{1,0:T(8,128)(2,1)S(1)} fusion(bf16[32768,128]{1,0:T(8,128)(2,1)} %bitcast.314, bf16[64,128]{1,0:T(8,128)(2,1)S(1)} %fusion.65, s32[1,64,32768]{2,1,0:T(8,128)} %param.10, f32[128]{0:T(128)S(1)} %copy-done.2), kind=kOutput, calls=%fused_computation.118 | convolution fusion | flops 1080680448 | bytes 16810496 | tf_op jit(solution)/shard_map/dot_general | solution.py:121
  174.6 12.4 %fusion.15 = f32[64,128]{1,0:T(8,128)S(1)} fusion(bf16[32768,128]{1,0:T(8,128)(2,1)} %bitcast.315, bf16[64,128]{1,0:T(8,128)(2,1)S(1)} %fusion.69, s32[1,64,32768]{2,1,0:T(8,128)} %param.10, f32[128]{0:T(128)S(1)} %copy-done.2), kind=kOutput, calls=%fused_computation.35 | convolution fusion | flops 1080057856 | bytes 16826880 | tf_op jit(solution)/shard_map/dot_general | solution.py:121
  186.9 9.2 %fusion.3 = bf16[64,32768]{1,0:T(8,128)(2,1)S(1)} fusion(bf16[32768,128]{1,0:T(8,128)(2,1)} %bitcast.316, s32[1,64,32768]{2,1,0:T(8,128)} %param.10, f32[64,128]{1,0:T(8,128)S(1)} %fusion.15), kind=kOutput, calls=%fused_computation.11 | convolution fusion | flops 543784960 | bytes 21004288 | tf_op jit(solution)/shard_map/dot_general | solution.py:117
  198.1 7.3 %fusion.2 = bf16[32768,128]{1,0:T(8,128)(2,1)} fusion(bf16[64,32768]{1,0:T(8,128)(2,1)S(1)} %fusion.3, bf16[32768,128]{1,0:T(8,128)(2,1)} %bitcast.317, f32[64,128]{1,0:T(8,128)S(1)} %fusion.15), kind=kOutput, calls=%fused_computation.9 | convolution fusion | flops 550076416 | bytes 21004288 | tf_op jit(solution)/shard_map/dot_general | solution.py:128
  206.1 7.0 %add_bitcast_fusion = (f32[1,64,128]{2,1,0:T(8,128)}, f32[128]{0:T(128)S(1)}) fusion(f32[128]{0:T(128)S(1)} %copy-done.2, bf16[64,32768]{1,0:T(8,128)(2,1)} %copy-done, bf16[32768,128]{1,0:T(8,128)(2,1)} %bitcast.318, f32[64,128]{1,0:T(8,128)S(1)} %fusion.15), kind=kOutput, calls=%fused_computation.134 | convolution fusion | flops 537526144 | bytes 12649472 | tf_op jit(solution)/shard_map/dot_general | solution.py:121
  213.2 66.8 %psum.7 = f32[8,128]{1,0:T(8,128)S(1)} all-reduce(f32[8,128]{1,0:T(8,128)S(1)} %broadcast_multiply_fusion), channel_id=1, replica_groups=mesh['tm_0'=4,'tm_1'=2,'docs'=16] {'tm_0','tm_1','docs'}, use_global_device_ids=true, to_apply=%region_5.6 | all-reduce | flops 1024 | bytes 8192 | tf_op jit(solution)/shard_map/psum | solution.py:140
  281.2 22.2 %reduce-scatter.2.cloned.1.call-done = bf16[2048,128]{1,0:T(8,128)(2,1)} async-done(((bf16[32768,128]{1,0:T(8,128)(2,1)}), bf16[2048,128]{1,0:T(8,128)(2,1)}) %reduce-scatter.2.cloned.1.call-update) | async-done | bytes 524304 | tf_op jit(solution)/shard_map/reduce_scatter | solution.py:125
  303.4 2.1 fusion.52
  305.6 4.6 %all-gather.10 = bf16[2,1,128]{2,1,0:T(2,128)(2,1)S(1)} all-gather(bf16[1,1,128]{2,1,0:T(2,128)(2,1)S(1)} %get-tuple-element.221), channel_id=5, replica_groups=mesh['tm_0'=4,'tm_1'=2,'docs'=16] {'tm_1'}, dimensions={0}, use_global_device_ids=true | all-gather | bytes 768 | tf_op jit(solution)/shard_map/all_gather | solution.py:38
  310.2 21.5 %all-gather.21.cloned.1.call-done = bf16[4096,128]{1,0:T(8,128)(2,1)} async-done(((bf16[2048,128]{1,0:T(8,128)(2,1)}), bf16[4096,128]{1,0:T(8,128)(2,1)}) %all-gather.21.cloned.1.call-update) | async-done | bytes 1048592 | tf_op jit(solution)/shard_map/all_gather | solution.py:38
  331.7 2.2 fusion.33
  334.0 7.9 %all-gather.11 = bf16[4,1,128]{2,1,0:T(2,128)(2,1)S(1)} all-gather(bf16[1,1,128]{2,1,0:T(2,128)(2,1)S(1)} %get-tuple-element.216), channel_id=1, replica_groups=mesh['tm_0'=4,'tm_1'=2,'docs'=16] {'tm_0'}, dimensions={0}, use_global_device_ids=true | all-gather | bytes 1280 | tf_op jit(solution)/shard_map/all_gather | solution.py:38
  341.9 22.6 %all-gather.17.cloned.1.call-done = bf16[4,2048,128]{2,1,0:T(8,128)(2,1)} async-done(((bf16[1,2048,128]{2,1,0:T(8,128)(2,1)}), bf16[4,2048,128]{2,1,0:T(8,128)(2,1)}) %all-gather.17.cloned.1.call-update) | async-done | bytes 2097168 | tf_op jit(solution)/shard_map/all_gather | solution.py:38
  364.5 3.9 fusion.313
  368.6 4.6 %all-gather.8 = bf16[2,1,128]{2,1,0:T(2,128)(2,1)S(1)} all-gather(bf16[1,1,128]{2,1,0:T(2,128)(2,1)S(1)} %get-tuple-element.218), channel_id=4, replica_groups=mesh['tm_0'=4,'tm_1'=2,'docs'=16] {'tm_1'}, dimensions={0}, use_global_device_ids=true | all-gather | bytes 768 | tf_op jit(solution)/shard_map/all_gather | solution.py:59
  373.2 20.7 %all-gather.23.cloned.1.call-done = bf16[4096,128]{1,0:T(8,128)(2,1)} async-done(((bf16[2048,128]{1,0:T(8,128)(2,1)}), bf16[4096,128]{1,0:T(8,128)(2,1)}) %all-gather.23.cloned.1.call-update) | async-done | bytes 1048592 | tf_op jit(solution)/shard_map/all_gather | solution.py:59
  393.8 2.2 fusion.37
  396.1 7.9 %all-gather.9 = bf16[4,1,128]{2,1,0:T(2,128)(2,1)S(1)} all-gather(bf16[1,1,128]{2,1,0:T(2,128)(2,1)S(1)} %get-tuple-element.212), channel_id=1, replica_groups=mesh['tm_0'=4,'tm_1'=2,'docs'=16] {'tm_0'}, dimensions={0}, use_global_device_ids=true | all-gather | bytes 1280 | tf_op jit(solution)/shard_map/all_gather | solution.py:59
  404.0 22.7 %all-gather.19.cloned.1.call-done = bf16[4,2048,128]{2,1,0:T(8,128)(2,1)} async-done(((bf16[1,2048,128]{2,1,0:T(8,128)(2,1)}), bf16[4,2048,128]{2,1,0:T(8,128)(2,1)}) %all-gather.19.cloned.1.call-update) | async-done | bytes 2097168 | tf_op jit(solution)/shard_map/all_gather | solution.py:59
  426.7 3.7 fusion.24
  (89 shorter events, 11.8 us)
Async XLA Ops:
  7.2 296.3 %reduce-scatter.2.cloned.1.call-start = ((), (), s32[]{:S(2)}) async-start(), calls=%async_computation.2 | async-start | bytes 8912896 | tf_op jit(solution)/shard_map/reduce_scatter | solution.py:125
  51.4 97.5 %copy-start.2 = (f32[128]{0:T(128)S(1)}, f32[128]{0:T(128)}, u32[]{:S(2)}) copy-start(f32[128]{0:T(128)} %param.13) | copy-start | bytes 1540
  51.4 97.5 %copy-start.5 = (f32[1,64,128]{2,1,0:T(8,128)S(1)}, f32[1,64,128]{2,1,0:T(8,128)}, u32[]{:S(2)}) copy-start(f32[1,64,128]{2,1,0:T(8,128)} %param.12) | copy-start | bytes 98308
  196.2 1.9 copy-start
  205.4 0.7 copy-start.1
  205.4 126.3 %all-gather.21.cloned.1.call-start = ((), (), s32[]{:S(2)}) async-start(), calls=%async_computation.5 | async-start | bytes 1572864 | tf_op jit(solution)/shard_map/all_gather | solution.py:38
  206.1 74.1 %copy-start.3 = (f32[128]{0:T(128)S(1)}, f32[128]{0:T(128)}, u32[]{:S(2)}) copy-start(f32[128]{0:T(128)} %param.15) | copy-start | bytes 1540
  206.1 75.0 %copy-start.4 = (pred[8]{0:T(512)(128)(4,1)S(1)}, pred[8]{0:T(512)(128)(4,1)}, u32[]{:S(2)}) copy-start(pred[8]{0:T(512)(128)(4,1)} %constant.117.clone.1) | copy-start | bytes 28
  305.5 59.0 %all-gather.17.cloned.1.call-start = ((), (), s32[]{:S(2)}) async-start(), calls=%async_computation.3 | async-start | bytes 2621440 | tf_op jit(solution)/shard_map/all_gather | solution.py:38
  333.9 59.9 %all-gather.23.cloned.1.call-start = ((), (), s32[]{:S(2)}) async-start(), calls=%async_computation.6 | async-start | bytes 1572864 | tf_op jit(solution)/shard_map/all_gather | solution.py:59
  368.5 58.1 %all-gather.19.cloned.1.call-start = ((), (), s32[]{:S(2)}) async-start(), calls=%async_computation.4 | async-start | bytes 2621440 | tf_op jit(solution)/shard_map/all_gather | solution.py:59
Sparse Core Ops, SparseCore 0:
  205.6 97.8 reduce-scatter.1
  305.7 26.0 all-gather.20
  334.1 30.4 all-gather.16
  368.6 25.1 all-gather.22
  396.2 30.4 all-gather.18
